TPU v7x, 32 devices: a whole 2x2x4 slice. The times are simulated.
32 devices in a mesh: row: 8 (over y, x, core), col: 4 (over z).
Axes of the slice: x: 2, y: 2, z: 4, core: 2. Of those that a mesh axis runs over, the one named last changes fastest.
Arguments:
- left_panels: float32 [8, 4, 16, 128, 128], P('row', 'col'), may hold values from -6 to 6
- right_panels: float32 [2, 4, 8, 12, 128, 128], P(None, 'col', 'row'), may hold values from -0.25 to 0.25
- product_lists: int32 [8, 4, 8, 96, 3], P('row', 'col'), may hold values from -1 to 23, as said below
Outputs:
- product_blocks: float32 [8, 4, 24, 128, 128], P('row', 'col')
Inputs may be any that keep to these rules, and one draw needn't show every extreme that they name: `product_lists`: each entry is (left slot < 16, right slot < 12, output slot < 24). In each list the first entries, at least half of 96 and at most 96, are live with distinct (left, right) pairs, the rest are -1 in all three columns; some list holds 96 live entries.
All inputs are finite; a program needn't handle non-finite values.
Results may differ from a plain program's by a relative error of at most 0.0003.
Values sent between devices are 32-bit elements; how exact they have to be, the bound alone decides.
A program may use at most 128 MiB of HBM per device.

v0:
```python
import jax
import jax.numpy as jnp
from jax import lax
from jax.sharding import PartitionSpec as P

BLK = 128
OCAP = 24


def contribute(left_stack, right_panel, entries, slot_count):
    live_mask = entries[:, 0] >= 0
    left_slot = jnp.maximum(entries[:, 0], 0)
    right_slot = jnp.maximum(entries[:, 1], 0)
    taken_left = jnp.take(left_stack, left_slot, axis=0)
    taken_right = jnp.take(right_panel, right_slot, axis=0)
    blocks = jnp.einsum("pik,pkj->pij", taken_left, taken_right, precision=lax.Precision.HIGHEST)
    slot_ids = jnp.arange(slot_count, dtype=jnp.int32)
    onehot = ((entries[:, 2][None, :] == slot_ids[:, None]) & live_mask[None, :]).astype(
        blocks.dtype
    )
    return jnp.einsum("op,pij->oij", onehot, blocks, precision=lax.Precision.HIGHEST)


def shards(left_panels, right_panels, product_lists):
    row_count = lax.axis_size("row")
    col_count = lax.axis_size("col")
    row_pos = lax.axis_index("row")
    col_pos = lax.axis_index("col")
    entries = product_lists[0, 0]
    step_count = entries.shape[0]
    running = jnp.zeros((OCAP, BLK, BLK), jnp.float32)
    right_all = lax.all_gather(right_panels, "col", axis=1, tiled=True)
    pieces = lax.all_gather(left_panels, "row", axis=0, tiled=True)

    def one_row(offset, partial_value):
        step_num = (offset - row_pos - col_pos) % row_count
        left_stack = lax.dynamic_index_in_dim(pieces, offset, 0, keepdims=False)[0]
        right_panel = right_all[offset // col_count, offset % col_count, 0]
        entry_rows = lax.dynamic_index_in_dim(
            entries, jnp.minimum(step_num, step_count - 1), 0, keepdims=False
        )
        return lax.cond(
            step_num < step_count,
            lambda inner: inner + contribute(left_stack, right_panel, entry_rows, OCAP),
            lambda inner: inner,
            partial_value,
        )

    running = lax.fori_loop(0, pieces.shape[0], one_row, running)
    return running[None, None]


def solution(mesh):
    return jax.shard_map(
        shards,
        mesh=mesh,
        in_specs=(
            P("row", "col", None, None, None),
            P(None, "col", "row", None, None, None),
            P("row", "col", None, None, None),
        ),
        out_specs=P("row", "col", None, None, None),
        check_vma=False,
    )
```

profile of v0, /device:TPU:0, one launch (start us, length us, event | category | flops | bytes accessed | tf_op | source)
XLA Modules:
  0.0 394.5 jit_solution(15243626719083775768)
XLA Ops:
  8.7 118.3 %all-gather.5.cloned.1.call-done = f32[2,4,1,12,128,128]{5,4,3,2,1,0:T(8,128)} async-done(((f32[2,1,1,12,128,128]{5,4,3,2,1,0:T(8,128)}), f32[2,4,1,12,128,128]{5,4,3,2,1,0:T(8,128)}) %all-gather.5.cloned.1.call-update) | async-done | bytes 6291472 | tf_op jit(solution)/shard_map/all_gather | solution.py:32
  127.0 54.4 %all-gather.3.cloned.1.call-done = f32[8,1,16,128,128]{4,3,2,1,0:T(8,128)} async-done(((f32[1,1,16,128,128]{4,3,2,1,0:T(8,128)}), f32[8,1,16,128,128]{4,3,2,1,0:T(8,128)}) %all-gather.3.cloned.1.call-update) | async-done | bytes 8388624 | tf_op jit(solution)/shard_map/all_gather | solution.py:33
  181.5 204.8 %while.19 = (s32[]{:T(128)}, f32[24,128,128]{2,0,1:T(8,128)S(1)}, s32[]{:T(128)}, s32[]{:T(128)}, s32[8,96,3]{1,2,0:T(4,128)S(1)}, /*index=5*/f32[8,1,16,128,128...) while((s32[]{:T(128)}, f32[24,128,128]{2,0,1:T(8,128)S(1)}, ...), condition=%wide.region_3.4_spmd, body=%wide.region_0.3_spmd.sunk | while | flops 2872450304 | bytes 57164012 | solution.py:49
  181.5 25.6 %conditional.2 = (f32[24,128,128]{2,0,1:T(8,128)S(1)}) conditional(s32[]{:T(128)} %convert_element_type.13, f32[24,128,128]{2,0,1:T(8,128)S(1)} %get-tuple-element.574, (s32[]{:T(128)}, s32[8,96,3]{1,2,0:T(4,128)S(1)}, s32[]{:T(128)}, f32[8,1,16,128,128]{4,3,2,1,0:T(8,128)}, f32[2,4,1,12,128,128]{5,4,3,2,1,0:T(8,128)}, ...), branch_computations={%region_1.1_spmd, %region_2.2_spmd} | conditional | flops 2872450304 | bytes 57163708 | solution.py:42
  182.8 3.5 gather_fusion.1
  186.3 1.3 dynamic-slice_bitcast_fusion
  187.6 3.6 gather_fusion
  191.2 9.5 %fusion.2 = f32[96,128,128]{2,1,0:T(8,128)S(1)} fusion(f32[96,128,128]{2,1,0:T(8,128)} %gather_fusion.1, f32[96,128,128]{2,1,0:T(8,128)} %gather_fusion, pred[96]{0:T(512)(128)(4,1)S(1)} %get-tuple-element.513, pred[96]{0:T(512)(128)(4,1)S(1)} %get-tuple-element.512), kind=kOutput, calls=%fused_computation.4 | convolution fusion | flops 2419064832 | bytes 18874560 | tf_op jit(solution)/shard_map/while/body/eval_jaxpr/cond/branch_1_fun/pik,pkj->pij/dot_general | solution.py:16
  200.8 6.3 %fusion.8 = f32[24,128,128]{2,0,1:T(8,128)S(1)} fusion(f32[24,128,128]{2,0,1:T(8,128)S(1)} %get-tuple-element.481, f32[96,128,128]{2,1,0:T(8,128)S(1)} %fusion.2, s32[96]{0:T(128)S(1)} %get-tuple-element.514, pred[96]{0:T(512)(128)(4,1)S(1)} %get-tuple-element.511), kind=kOutput, calls=%fused_computation.10 | convolution fusion | flops 453382656 | bytes 9437664 | tf_op jit(solution)/shard_map/while/body/eval_jaxpr/cond/branch_1_fun/op,pij->oij/dot_general | solution.py:21
  207.1 25.6 %conditional.2 = (f32[24,128,128]{2,0,1:T(8,128)S(1)}) conditional(s32[]{:T(128)} %convert_element_type.13, f32[24,128,128]{2,0,1:T(8,128)S(1)} %get-tuple-element.574, (s32[]{:T(128)}, s32[8,96,3]{1,2,0:T(4,128)S(1)}, s32[]{:T(128)}, f32[8,1,16,128,128]{4,3,2,1,0:T(8,128)}, f32[2,4,1,12,128,128]{5,4,3,2,1,0:T(8,128)}, ...), branch_computations={%region_1.1_spmd, %region_2.2_spmd} | conditional | flops 2872450304 | bytes 57163708 | solution.py:42
  208.4 3.5 gather_fusion.1
  213.2 3.6 gather_fusion
  216.8 9.5 %fusion.2 = f32[96,128,128]{2,1,0:T(8,128)S(1)} fusion(f32[96,128,128]{2,1,0:T(8,128)} %gather_fusion.1, f32[96,128,128]{2,1,0:T(8,128)} %gather_fusion, pred[96]{0:T(512)(128)(4,1)S(1)} %get-tuple-element.513, pred[96]{0:T(512)(128)(4,1)S(1)} %get-tuple-element.512), kind=kOutput, calls=%fused_computation.4 | convolution fusion | flops 2419064832 | bytes 18874560 | tf_op jit(solution)/shard_map/while/body/eval_jaxpr/cond/branch_1_fun/pik,pkj->pij/dot_general | solution.py:16
  226.4 6.3 %fusion.8 = f32[24,128,128]{2,0,1:T(8,128)S(1)} fusion(f32[24,128,128]{2,0,1:T(8,128)S(1)} %get-tuple-element.481, f32[96,128,128]{2,1,0:T(8,128)S(1)} %fusion.2, s32[96]{0:T(128)S(1)} %get-tuple-element.514, pred[96]{0:T(512)(128)(4,1)S(1)} %get-tuple-element.511), kind=kOutput, calls=%fused_computation.10 | convolution fusion | flops 453382656 | bytes 9437664 | tf_op jit(solution)/shard_map/while/body/eval_jaxpr/cond/branch_1_fun/op,pij->oij/dot_general | solution.py:21
  232.7 25.6 %conditional.2 = (f32[24,128,128]{2,0,1:T(8,128)S(1)}) conditional(s32[]{:T(128)} %convert_element_type.13, f32[24,128,128]{2,0,1:T(8,128)S(1)} %get-tuple-element.574, (s32[]{:T(128)}, s32[8,96,3]{1,2,0:T(4,128)S(1)}, s32[]{:T(128)}, f32[8,1,16,128,128]{4,3,2,1,0:T(8,128)}, f32[2,4,1,12,128,128]{5,4,3,2,1,0:T(8,128)}, ...), branch_computations={%region_1.1_spmd, %region_2.2_spmd} | conditional | flops 2872450304 | bytes 57163708 | solution.py:42
  234.0 3.5 gather_fusion.1
  238.8 3.6 gather_fusion
  242.4 9.5 %fusion.2 = f32[96,128,128]{2,1,0:T(8,128)S(1)} fusion(f32[96,128,128]{2,1,0:T(8,128)} %gather_fusion.1, f32[96,128,128]{2,1,0:T(8,128)} %gather_fusion, pred[96]{0:T(512)(128)(4,1)S(1)} %get-tuple-element.513, pred[96]{0:T(512)(128)(4,1)S(1)} %get-tuple-element.512), kind=kOutput, calls=%fused_computation.4 | convolution fusion | flops 2419064832 | bytes 18874560 | tf_op jit(solution)/shard_map/while/body/eval_jaxpr/cond/branch_1_fun/pik,pkj->pij/dot_general | solution.py:16
  252.0 6.3 %fusion.8 = f32[24,128,128]{2,0,1:T(8,128)S(1)} fusion(f32[24,128,128]{2,0,1:T(8,128)S(1)} %get-tuple-element.481, f32[96,128,128]{2,1,0:T(8,128)S(1)} %fusion.2, s32[96]{0:T(128)S(1)} %get-tuple-element.514, pred[96]{0:T(512)(128)(4,1)S(1)} %get-tuple-element.511), kind=kOutput, calls=%fused_computation.10 | convolution fusion | flops 453382656 | bytes 9437664 | tf_op jit(solution)/shard_map/while/body/eval_jaxpr/cond/branch_1_fun/op,pij->oij/dot_general | solution.py:21
  258.3 25.6 %conditional.2 = (f32[24,128,128]{2,0,1:T(8,128)S(1)}) conditional(s32[]{:T(128)} %convert_element_type.13, f32[24,128,128]{2,0,1:T(8,128)S(1)} %get-tuple-element.574, (s32[]{:T(128)}, s32[8,96,3]{1,2,0:T(4,128)S(1)}, s32[]{:T(128)}, f32[8,1,16,128,128]{4,3,2,1,0:T(8,128)}, f32[2,4,1,12,128,128]{5,4,3,2,1,0:T(8,128)}, ...), branch_computations={%region_1.1_spmd, %region_2.2_spmd} | conditional | flops 2872450304 | bytes 57163708 | solution.py:42
  259.6 3.5 gather_fusion.1
  263.1 1.3 dynamic-slice_bitcast_fusion
  264.4 3.6 gather_fusion
  268.0 9.5 %fusion.2 = f32[96,128,128]{2,1,0:T(8,128)S(1)} fusion(f32[96,128,128]{2,1,0:T(8,128)} %gather_fusion.1, f32[96,128,128]{2,1,0:T(8,128)} %gather_fusion, pred[96]{0:T(512)(128)(4,1)S(1)} %get-tuple-element.513, pred[96]{0:T(512)(128)(4,1)S(1)} %get-tuple-element.512), kind=kOutput, calls=%fused_computation.4 | convolution fusion | flops 2419064832 | bytes 18874560 | tf_op jit(solution)/shard_map/while/body/eval_jaxpr/cond/branch_1_fun/pik,pkj->pij/dot_general | solution.py:16
  277.6 6.3 %fusion.8 = f32[24,128,128]{2,0,1:T(8,128)S(1)} fusion(f32[24,128,128]{2,0,1:T(8,128)S(1)} %get-tuple-element.481, f32[96,128,128]{2,1,0:T(8,128)S(1)} %fusion.2, s32[96]{0:T(128)S(1)} %get-tuple-element.514, pred[96]{0:T(512)(128)(4,1)S(1)} %get-tuple-element.511), kind=kOutput, calls=%fused_computation.10 | convolution fusion | flops 453382656 | bytes 9437664 | tf_op jit(solution)/shard_map/while/body/eval_jaxpr/cond/branch_1_fun/op,pij->oij/dot_general | solution.py:21
  283.9 25.6 %conditional.2 = (f32[24,128,128]{2,0,1:T(8,128)S(1)}) conditional(s32[]{:T(128)} %convert_element_type.13, f32[24,128,128]{2,0,1:T(8,128)S(1)} %get-tuple-element.574, (s32[]{:T(128)}, s32[8,96,3]{1,2,0:T(4,128)S(1)}, s32[]{:T(128)}, f32[8,1,16,128,128]{4,3,2,1,0:T(8,128)}, f32[2,4,1,12,128,128]{5,4,3,2,1,0:T(8,128)}, ...), branch_computations={%region_1.1_spmd, %region_2.2_spmd} | conditional | flops 2872450304 | bytes 57163708 | solution.py:42
  285.2 3.5 gather_fusion.1
  290.0 3.6 gather_fusion
  293.6 9.5 %fusion.2 = f32[96,128,128]{2,1,0:T(8,128)S(1)} fusion(f32[96,128,128]{2,1,0:T(8,128)} %gather_fusion.1, f32[96,128,128]{2,1,0:T(8,128)} %gather_fusion, pred[96]{0:T(512)(128)(4,1)S(1)} %get-tuple-element.513, pred[96]{0:T(512)(128)(4,1)S(1)} %get-tuple-element.512), kind=kOutput, calls=%fused_computation.4 | convolution fusion | flops 2419064832 | bytes 18874560 | tf_op jit(solution)/shard_map/while/body/eval_jaxpr/cond/branch_1_fun/pik,pkj->pij/dot_general | solution.py:16
  303.2 6.3 %fusion.8 = f32[24,128,128]{2,0,1:T(8,128)S(1)} fusion(f32[24,128,128]{2,0,1:T(8,128)S(1)} %get-tuple-element.481, f32[96,128,128]{2,1,0:T(8,128)S(1)} %fusion.2, s32[96]{0:T(128)S(1)} %get-tuple-element.514, pred[96]{0:T(512)(128)(4,1)S(1)} %get-tuple-element.511), kind=kOutput, calls=%fused_computation.10 | convolution fusion | flops 453382656 | bytes 9437664 | tf_op jit(solution)/shard_map/while/body/eval_jaxpr/cond/branch_1_fun/op,pij->oij/dot_general | solution.py:21
  309.5 25.6 %conditional.2 = (f32[24,128,128]{2,0,1:T(8,128)S(1)}) conditional(s32[]{:T(128)} %convert_element_type.13, f32[24,128,128]{2,0,1:T(8,128)S(1)} %get-tuple-element.574, (s32[]{:T(128)}, s32[8,96,3]{1,2,0:T(4,128)S(1)}, s32[]{:T(128)}, f32[8,1,16,128,128]{4,3,2,1,0:T(8,128)}, f32[2,4,1,12,128,128]{5,4,3,2,1,0:T(8,128)}, ...), branch_computations={%region_1.1_spmd, %region_2.2_spmd} | conditional | flops 2872450304 | bytes 57163708 | solution.py:42
  310.8 3.5 gather_fusion.1
  315.6 3.6 gather_fusion
  319.2 9.5 %fusion.2 = f32[96,128,128]{2,1,0:T(8,128)S(1)} fusion(f32[96,128,128]{2,1,0:T(8,128)} %gather_fusion.1, f32[96,128,128]{2,1,0:T(8,128)} %gather_fusion, pred[96]{0:T(512)(128)(4,1)S(1)} %get-tuple-element.513, pred[96]{0:T(512)(128)(4,1)S(1)} %get-tuple-element.512), kind=kOutput, calls=%fused_computation.4 | convolution fusion | flops 2419064832 | bytes 18874560 | tf_op jit(solution)/shard_map/while/body/eval_jaxpr/cond/branch_1_fun/pik,pkj->pij/dot_general | solution.py:16
  328.8 6.3 %fusion.8 = f32[24,128,128]{2,0,1:T(8,128)S(1)} fusion(f32[24,128,128]{2,0,1:T(8,128)S(1)} %get-tuple-element.481, f32[96,128,128]{2,1,0:T(8,128)S(1)} %fusion.2, s32[96]{0:T(128)S(1)} %get-tuple-element.514, pred[96]{0:T(512)(128)(4,1)S(1)} %get-tuple-element.511), kind=kOutput, calls=%fused_computation.10 | convolution fusion | flops 453382656 | bytes 9437664 | tf_op jit(solution)/shard_map/while/body/eval_jaxpr/cond/branch_1_fun/op,pij->oij/dot_general | solution.py:21
  335.1 25.6 %conditional.2 = (f32[24,128,128]{2,0,1:T(8,128)S(1)}) conditional(s32[]{:T(128)} %convert_element_type.13, f32[24,128,128]{2,0,1:T(8,128)S(1)} %get-tuple-element.574, (s32[]{:T(128)}, s32[8,96,3]{1,2,0:T(4,128)S(1)}, s32[]{:T(128)}, f32[8,1,16,128,128]{4,3,2,1,0:T(8,128)}, f32[2,4,1,12,128,128]{5,4,3,2,1,0:T(8,128)}, ...), branch_computations={%region_1.1_spmd, %region_2.2_spmd} | conditional | flops 2872450304 | bytes 57163708 | solution.py:42
  336.4 3.5 gather_fusion.1
  339.9 1.3 dynamic-slice_bitcast_fusion
  341.2 3.6 gather_fusion
  344.8 9.5 %fusion.2 = f32[96,128,128]{2,1,0:T(8,128)S(1)} fusion(f32[96,128,128]{2,1,0:T(8,128)} %gather_fusion.1, f32[96,128,128]{2,1,0:T(8,128)} %gather_fusion, pred[96]{0:T(512)(128)(4,1)S(1)} %get-tuple-element.513, pred[96]{0:T(512)(128)(4,1)S(1)} %get-tuple-element.512), kind=kOutput, calls=%fused_computation.4 | convolution fusion | flops 2419064832 | bytes 18874560 | tf_op jit(solution)/shard_map/while/body/eval_jaxpr/cond/branch_1_fun/pik,pkj->pij/dot_general | solution.py:16
  354.4 6.3 %fusion.8 = f32[24,128,128]{2,0,1:T(8,128)S(1)} fusion(f32[24,128,128]{2,0,1:T(8,128)S(1)} %get-tuple-element.481, f32[96,128,128]{2,1,0:T(8,128)S(1)} %fusion.2, s32[96]{0:T(128)S(1)} %get-tuple-element.514, pred[96]{0:T(512)(128)(4,1)S(1)} %get-tuple-element.511), kind=kOutput, calls=%fused_computation.10 | convolution fusion | flops 453382656 | bytes 9437664 | tf_op jit(solution)/shard_map/while/body/eval_jaxpr/cond/branch_1_fun/op,pij->oij/dot_general | solution.py:21
  360.7 25.6 %conditional.2 = (f32[24,128,128]{2,0,1:T(8,128)S(1)}) conditional(s32[]{:T(128)} %convert_element_type.13, f32[24,128,128]{2,0,1:T(8,128)S(1)} %get-tuple-element.574, (s32[]{:T(128)}, s32[8,96,3]{1,2,0:T(4,128)S(1)}, s32[]{:T(128)}, f32[8,1,16,128,128]{4,3,2,1,0:T(8,128)}, f32[2,4,1,12,128,128]{5,4,3,2,1,0:T(8,128)}, ...), branch_computations={%region_1.1_spmd, %region_2.2_spmd} | conditional | flops 2872450304 | bytes 57163708 | solution.py:42
  362.0 3.5 gather_fusion.1
  365.5 1.3 dynamic-slice_bitcast_fusion
  366.8 3.6 gather_fusion
  370.4 9.5 %fusion.2 = f32[96,128,128]{2,1,0:T(8,128)S(1)} fusion(f32[96,128,128]{2,1,0:T(8,128)} %gather_fusion.1, f32[96,128,128]{2,1,0:T(8,128)} %gather_fusion, pred[96]{0:T(512)(128)(4,1)S(1)} %get-tuple-element.513, pred[96]{0:T(512)(128)(4,1)S(1)} %get-tuple-element.512), kind=kOutput, calls=%fused_computation.4 | convolution fusion | flops 2419064832 | bytes 18874560 | tf_op jit(solution)/shard_map/while/body/eval_jaxpr/cond/branch_1_fun/pik,pkj->pij/dot_general | solution.py:16
  380.0 6.3 %fusion.8 = f32[24,128,128]{2,0,1:T(8,128)S(1)} fusion(f32[24,128,128]{2,0,1:T(8,128)S(1)} %get-tuple-element.481, f32[96,128,128]{2,1,0:T(8,128)S(1)} %fusion.2, s32[96]{0:T(128)S(1)} %get-tuple-element.514, pred[96]{0:T(512)(128)(4,1)S(1)} %get-tuple-element.511), kind=kOutput, calls=%fused_computation.10 | convolution fusion | flops 453382656 | bytes 9437664 | tf_op jit(solution)/shard_map/while/body/eval_jaxpr/cond/branch_1_fun/op,pij->oij/dot_general | solution.py:21
  386.3 1.4 copy.15
  (50 shorter events, 17.2 us)
Async XLA Ops:
  6.5 120.4 %all-gather.5.cloned.1.call-start = ((), (), s32[]{:S(2)}) async-start(), calls=%async_computation.1 | async-start | bytes 7864320 | tf_op jit(solution)/shard_map/all_gather | solution.py:32
  7.3 174.1 %all-gather.3.cloned.1.call-start = ((), (), s32[]{:S(2)}) async-start(), calls=%async_computation | async-start | bytes 9437184 | tf_op jit(solution)/shard_map/all_gather | solution.py:33
Sparse Core Ops, SparseCore 0:
  8.9 118.0 all-gather.4
  128.9 52.4 all-gather.2
where the time goes:
time: 395 us
  waiting for transfers between devices  174 us (44%)
  matrix products  127 us (32%)
  local copies, waits for them, and re-layouts  79.3 us (20%)
  between operations  13.4 us (3%)
    all_gather x1, waiting for transfers between devices, shards(): right_all = lax.all_gather(right_panels, 'col', axis=1, tiled=True)  118 us
    dot_general x8, matrix products, contribute(): jnp.einsum('pik,pkj->pij', taken_left, taken_right, precision=lax.Precisi...  76.2 us
    all_gather x1, waiting for transfers between devices, shards(): pieces = lax.all_gather(left_panels, 'row', axis=0, tiled=True)  54.4 us
    dot_general x8, matrix products, contribute(): jnp.einsum('op,pij->oij', onehot, blocks, precision=lax.Precision.HIGHEST)  50.3 us
    gather x8, local copies, waits for them, and re-layouts, contribute(): taken_left = jnp.take(left_stack, left_slot, axis=0)  28.9 us
    gather x8, local copies, waits for them, and re-layouts, contribute(): taken_right = jnp.take(right_panel, right_slot, axis=0)  28.2 us
    squeeze x8, local copies, waits for them, and re-layouts, one_row(): left_stack = lax.dynamic_index_in_dim(pieces, offset, 0, keepdims=False)[0]  10.3 us
    squeeze x8, local copies, waits for them, and re-layouts, one_row(): right_panel = right_all[offset // col_count, offset % col_count, 0]  9.53 us
  transfers between devices with their start and end apart: 2, of which 2 were waited for; matrix products, arithmetic and copies ran while one was open for 0% of the time, Pallas kernels for 0%

commit v1 on v0

v1 whole, which is shorter than its diff:
```python
import functools

import jax
import jax.numpy as jnp
from jax import lax
from jax.experimental import pallas as pl
from jax.experimental.pallas import tpu as pltpu
from jax.sharding import PartitionSpec as P

OCAP = 24
UNROLL = 8
AHEAD = 3
MESH = pl.DeviceIdType.MESH


def prepare(entries, slot_count):
    count = entries.shape[1]
    live = entries[..., 0] >= 0
    slots = jnp.where(live, entries[..., 2], slot_count)
    key = slots * count + jnp.arange(count, dtype=jnp.int32)
    rank = jnp.sum((key[:, None, :] < key[:, :, None]).astype(jnp.int32), axis=2)
    place = rank[:, None, :] == jnp.arange(count, dtype=jnp.int32)[None, :, None]

    def arrange(values):
        return jnp.sum(jnp.where(place, values[:, None, :], 0), axis=2)

    left_slot = arrange(jnp.maximum(entries[..., 0], 0))
    right_slot = arrange(jnp.maximum(entries[..., 1], 0))
    out_slot = arrange(slots)
    before = jnp.concatenate([jnp.full_like(out_slot[:, :1], -1), out_slot[:, :-1]], axis=1)
    keep = (out_slot == before).astype(jnp.int32)
    ids = jnp.arange(slot_count, dtype=jnp.int32)[None, :, None]
    upto = jnp.sum((slots[:, None, :] <= ids).astype(jnp.int32), axis=2)
    here = jnp.sum((slots[:, None, :] == ids).astype(jnp.int32), axis=2)
    last = jnp.maximum(upto - 1, 0)
    valid = (here > 0).astype(jnp.int32)
    return left_slot, right_slot, keep, last, valid


def kernel(row_count, col_count, a_ref, b_ref, keep_ref, last_ref, valid_ref, left_ref, right_ref, out_ref,
           left_all, right_all, lhs, rhs, sums, zsend, zrecv, lsend, psend, lrecv, local_sem):
    row = lax.axis_index("row")
    col = lax.axis_index("col")
    q_count = right_ref.shape[0]
    left_blocks, blk = left_ref.shape[2], left_ref.shape[3]
    right_blocks = right_ref.shape[3]
    step_count, pair_count = a_ref.shape
    slot_count = last_ref.shape[1]
    groups = row_count // 2
    group, parity = row // 2, row % 2
    partner = group * 2 + 1 - parity

    barrier = pltpu.get_barrier_semaphore()
    for i in range(1, groups):
        peer = lax.rem(group + i, groups) * 2 + parity
        pl.semaphore_signal(barrier, inc=1, device_id=(peer, col), device_id_type=MESH)
    pl.semaphore_signal(barrier, inc=1, device_id=(partner, col), device_id_type=MESH)

    @pl.when(col > 0)
    def _():
        pl.semaphore_signal(barrier, inc=1, device_id=(row, col - 1), device_id_type=MESH)

    @pl.when(col < col_count - 1)
    def _():
        pl.semaphore_signal(barrier, inc=1, device_id=(row, col + 1), device_id_type=MESH)

    own = [pltpu.make_async_copy(left_ref.at[0, 0], left_all.at[row], local_sem.at[0])]
    for q in range(q_count):
        own.append(pltpu.make_async_copy(right_ref.at[q, 0, 0], right_all.at[q, col], local_sem.at[1 + q]))
    for copy in own:
        copy.start()

    ends = (col == 0).astype(jnp.int32) + (col == col_count - 1).astype(jnp.int32)
    pl.semaphore_wait(barrier, groups + 2 - ends)

    def along(direction, q, source, from_ref):
        return pltpu.make_async_remote_copy(
            src_ref=from_ref,
            dst_ref=right_all.at[q, source],
            send_sem=zsend.at[direction, q, source],
            recv_sem=zrecv.at[q, source],
            device_id=(row, col + (1 if direction else -1)),
            device_id_type=MESH,
        )

    def own_panel(direction, q):
        return along(direction, q, col, right_ref.at[q, 0, 0])

    def relayed(direction, q, source):
        return along(direction, q, source, right_all.at[q, source])

    def across(i):
        return pltpu.make_async_remote_copy(
            src_ref=left_ref.at[0, 0],
            dst_ref=left_all.at[row],
            send_sem=lsend.at[i],
            recv_sem=lrecv.at[row],
            device_id=(lax.rem(group + i, groups) * 2 + parity, col),
            device_id_type=MESH,
        )

    def handed(i):
        source = lax.rem(group + i, groups) * 2 + parity
        return pltpu.make_async_remote_copy(
            src_ref=left_ref.at[0, 0] if i == 0 else left_all.at[source],
            dst_ref=left_all.at[source],
            send_sem=psend.at[i],
            recv_sem=lrecv.at[source],
            device_id=(partner, col),
            device_id_type=MESH,
        )

    def arrived_left(source):
        return pltpu.make_async_remote_copy(
            src_ref=left_all.at[source],
            dst_ref=left_all.at[source],
            send_sem=psend.at[0],
            recv_sem=lrecv.at[source],
            device_id=(partner, col),
            device_id_type=MESH,
        )

    for q in range(q_count):
        @pl.when(col > 0)
        def _():
            own_panel(0, q).start()

        @pl.when(col < col_count - 1)
        def _():
            own_panel(1, q).start()

    for i in range(1, groups):
        across(i).start()
    handed(0).start()

    out_ref[...] = jnp.zeros_like(out_ref)
    rhs[:, blk:, blk:] = jnp.zeros((right_blocks, blk, blk), rhs.dtype)
    for copy in own:
        copy.wait()

    sides = jnp.minimum(col, col_count - 1 - col)

    def source_of(position):
        rest = position - 1
        distance = jnp.where(rest < 2 * sides, rest // 2 + 1, rest - sides + 1)
        lower = jnp.where(rest < 2 * sides, rest % 2 == 0, col * 2 > col_count - 1)
        shifted = jnp.where(lower, col - distance, col + distance)
        return jnp.where(position == 0, col, shifted)

    def relay(item):
        source, q = source_of(item // q_count), lax.rem(item, q_count)

        @pl.when(source != col)
        def _():
            relayed(0, q, source).wait_recv()

        @pl.when((source < col) & (col < col_count - 1))
        def _():
            relayed(1, q, source).start()

        @pl.when((source > col) & (col > 0))
        def _():
            relayed(0, q, source).start()

    first = min(2 * q_count, row_count)
    lax.fori_loop(q_count, first, lambda item, c: (relay(item), c)[1], 0)
    for i in range(1, groups):
        source = lax.rem(group + i, groups) * 2 + parity
        arrived_left(source).wait_recv()
        handed(i).start()
    for i in range(groups):
        arrived_left(lax.rem(group + i, groups) * 2 + 1 - parity).wait_recv()

    def job(item, carry):
        ahead = item + AHEAD

        @pl.when((ahead >= first) & (ahead < row_count))
        def _():
            relay(ahead)

        source, q = source_of(item // q_count), lax.rem(item, q_count)
        kgroup = q * col_count + source
        step = lax.rem(kgroup - row - col + 2 * row_count, row_count)

        @pl.when(step < step_count)
        def _():
            def split_left(i, c):
                x = left_all[kgroup, i]
                high = x.astype(jnp.bfloat16)
                lhs[i, :, :blk] = high
                lhs[i, :, blk:] = (x - high.astype(jnp.float32)).astype(jnp.bfloat16)
                return c

            def split_right(i, c):
                x = right_all[q, source, i]
                high = x.astype(jnp.bfloat16)
                rhs[i, :blk, :blk] = high
                rhs[i, blk:, :blk] = high
                rhs[i, :blk, blk:] = (x - high.astype(jnp.float32)).astype(jnp.bfloat16)
                return c

            lax.fori_loop(0, left_blocks, split_left, 0)
            lax.fori_loop(0, right_blocks, split_right, 0)

            def some(batch, total):
                for u in range(UNROLL):
                    p = batch * UNROLL + u
                    both = jnp.dot(lhs[a_ref[step, p]], rhs[b_ref[step, p]], preferred_element_type=jnp.float32)
                    total = total * keep_ref[step, p].astype(jnp.float32) + (both[:, :blk] + both[:, blk:])
                    sums[p] = total
                return total

            lax.fori_loop(0, pair_count // UNROLL, some, jnp.zeros((blk, blk), jnp.float32))

            def put(o, c):
                out_ref[o] = out_ref[o] + sums[last_ref[step, o]] * valid_ref[step, o].astype(jnp.float32)
                return c

            lax.fori_loop(0, slot_count, put, 0)

        return carry

    lax.fori_loop(0, row_count, job, 0)

    for q in range(q_count):
        @pl.when(col > 0)
        def _():
            own_panel(0, q).wait_send()

        @pl.when(col < col_count - 1)
        def _():
            own_panel(1, q).wait_send()

    def sent(item, carry):
        source, q = source_of(item // q_count), lax.rem(item, q_count)

        @pl.when((source < col) & (col < col_count - 1))
        def _():
            relayed(1, q, source).wait_send()

        @pl.when((source > col) & (col > 0))
        def _():
            relayed(0, q, source).wait_send()

        return carry

    lax.fori_loop(q_count, row_count, sent, 0)
    for i in range(1, groups):
        across(i).wait_send()
    for i in range(groups):
        handed(i).wait_send()


def shards(row_count, col_count, left_panels, right_panels, product_lists):
    left_blocks, blk = left_panels.shape[2], left_panels.shape[3]
    q_count, right_blocks = right_panels.shape[0], right_panels.shape[3]
    pair_count = product_lists.shape[3]
    lists = prepare(product_lists[0, 0], OCAP)
    groups = row_count // 2
    out = pl.pallas_call(
        functools.partial(kernel, row_count, col_count),
        out_shape=jax.ShapeDtypeStruct((OCAP, blk, blk), jnp.float32),
        in_specs=[pl.BlockSpec(memory_space=pltpu.SMEM)] * 5 + [pl.BlockSpec(memory_space=pl.ANY)] * 2,
        out_specs=pl.BlockSpec(memory_space=pltpu.VMEM),
        scratch_shapes=[
            pltpu.VMEM((row_count, left_blocks, blk, blk), jnp.float32),
            pltpu.VMEM((q_count, col_count, right_blocks, blk, blk), jnp.float32),
            pltpu.VMEM((left_blocks, blk, 2 * blk), jnp.bfloat16),
            pltpu.VMEM((right_blocks, 2 * blk, 2 * blk), jnp.bfloat16),
            pltpu.VMEM((pair_count, blk, blk), jnp.float32),
            pltpu.SemaphoreType.DMA((2, q_count, col_count)),
            pltpu.SemaphoreType.DMA((q_count, col_count)),
            pltpu.SemaphoreType.DMA((groups,)),
            pltpu.SemaphoreType.DMA((groups,)),
            pltpu.SemaphoreType.DMA((row_count,)),
            pltpu.SemaphoreType.DMA((1 + q_count,)),
        ],
        compiler_params=pltpu.CompilerParams(
            collective_id=0, has_side_effects=True, vmem_limit_bytes=60 * 1024 * 1024
        ),
    )(*lists, left_panels, right_panels)
    return out[None, None]


def solution(mesh):
    return jax.shard_map(
        functools.partial(shards, mesh.shape["row"], mesh.shape["col"]),
        mesh=mesh,
        in_specs=(
            P("row", "col", None, None, None),
            P(None, "col", "row", None, None, None),
            P("row", "col", None, None, None),
        ),
        out_specs=P("row", "col", None, None, None),
        check_vma=False,
    )
```

time: 395 us -> 158 us (0.40)
  waiting for transfers between devices: 174 us -> 0 us
  Pallas kernels: 0 us -> 150 us
  matrix products: 127 us -> 0 us
  local copies, waits for them, and re-layouts: 79.3 us -> 2.7 us
  between operations: 13.4 us -> 0.02 us
  other arithmetic: 0.16 us -> 5.06 us
    all_gather x2 -> x0, waiting for transfers between devices: 173 us -> none  [the longest x1 118 us: shards(): right_all = lax.all_gather(right_panels, 'col', axis=1, tiled=True)]
    pallas_call x0 -> x1, Pallas kernels: none -> 150 us  [shards(): pl.pallas_call(functools.partial(kernel, row_count, col_count), out_shape...]
    dot_general x16 -> x0, matrix products: 127 us -> none  [the longest x8 76.2 us: contribute(): jnp.einsum('pik,pkj->pij', taken_left, taken_right, precision=lax.Precisi...]
    gather x16 -> x0, local copies, waits for them, and re-layouts: 57.1 us -> none  [the longest x8 28.9 us: contribute(): taken_left = jnp.take(left_stack, left_slot, axis=0)]
    squeeze x24 -> x0, local copies, waits for them, and re-layouts: 19.9 us -> none  [the longest x8 10.3 us: one_row(): left_stack = lax.dynamic_index_in_dim(pieces, offset, 0, keepdims=False)[0]]
  transfers between devices with their start and end apart: 2 -> 0, of which waited for: 2 -> 0; matrix products, arithmetic and copies ran while one was open for 0% -> 0% of each run, Pallas kernels for 0% -> 0%
where the time goes in v1:
time: 158 us
  Pallas kernels  150 us (95%)
  other arithmetic  5.06 us (3%)
  local copies, waits for them, and re-layouts  2.7 us (2%)
    pallas_call x1, Pallas kernels, shards(): pl.pallas_call(functools.partial(kernel, row_count, col_count), out_shape...  150 us

profile of v1, /device:TPU:0, one launch (start us, length us, event | category | flops | bytes accessed | tf_op | source)
XLA Modules:
  0.0 157.6 jit_solution(16916219575692253640)
XLA Ops:
  0.0 0.7 iota_add_fusion
  0.7 0.3 convert_reduce_fusion.1
  1.1 0.6 compare_convert_fusion.valid_ref
  1.7 0.6 add_maximum_fusion.last_ref
  2.2 0.7 maximum_bitcast_fusion
  3.0 0.3 convert_reduce_fusion
  3.3 1.1 select_reduce_fusion
  4.4 0.7 fusion.1.keep_ref
  5.1 149.8 %shard_map.37 = f32[24,128,128]{2,1,0:T(8,128)} custom-call(s32[8,96]{1,0:T(8,128)} %get-tuple-element.9.a_ref, s32[8,96]{1,0:T(8,128)} %get-tuple-element.8.b_ref, s32[8,96]{1,0:T(8,128)} %fusion.1.keep_ref, s32[8,24]{1,0:T(8,128)} %add_maximum_fusion.last_ref, s32[8,24]{1,0:T(8,128)} %compare_convert_fusion.valid_ref, f32[1,1,16,128,128]{4,3,2,1,0:T(8,128)} %left_ref.1, ...), custom_call_target="tpu_custom_call" | custom-call | tf_op jit(solution)/shard_map/pallas_call | solution.py:260
  154.9 2.7 %copy.5 = f32[1,1,24,128,128]{4,3,2,1,0:T(8,128)} copy(f32[1,1,24,128,128]{4,3,2,1,0:T(8,128)} %bitcast.12) | data formatting | bytes 3145728

commit v2 on v1

--- a/solution.py
+++ b/solution.py
@@ -19,41 +19,39 @@
     slots = jnp.where(live, entries[..., 2], slot_count)
     key = slots * count + jnp.arange(count, dtype=jnp.int32)
     rank = jnp.sum((key[:, None, :] < key[:, :, None]).astype(jnp.int32), axis=2)
+    packed = jnp.where(live, entries[..., 0] + entries[..., 1] * 256, 0) + slots * 65536
     place = rank[:, None, :] == jnp.arange(count, dtype=jnp.int32)[None, :, None]
-
-    def arrange(values):
-        return jnp.sum(jnp.where(place, values[:, None, :], 0), axis=2)
-
-    left_slot = arrange(jnp.maximum(entries[..., 0], 0))
-    right_slot = arrange(jnp.maximum(entries[..., 1], 0))
-    out_slot = arrange(slots)
-    before = jnp.concatenate([jnp.full_like(out_slot[:, :1], -1), out_slot[:, :-1]], axis=1)
-    keep = (out_slot == before).astype(jnp.int32)
+    codes = jnp.sum(jnp.where(place, packed[:, None, :], 0), axis=2)
     ids = jnp.arange(slot_count, dtype=jnp.int32)[None, :, None]
-    upto = jnp.sum((slots[:, None, :] <= ids).astype(jnp.int32), axis=2)
-    here = jnp.sum((slots[:, None, :] == ids).astype(jnp.int32), axis=2)
-    last = jnp.maximum(upto - 1, 0)
-    valid = (here > 0).astype(jnp.int32)
-    return left_slot, right_slot, keep, last, valid
-
-
-def kernel(row_count, col_count, a_ref, b_ref, keep_ref, last_ref, valid_ref, left_ref, right_ref, out_ref,
-           left_all, right_all, lhs, rhs, sums, zsend, zrecv, lsend, psend, lrecv, local_sem):
+    upto = (slots[:, None, :] <= ids).astype(jnp.int32) + (slots[:, None, :] == ids).astype(jnp.int32) * 65536
+    return codes, jnp.sum(upto, axis=2)
+
+
+def kernel(row_count, col_count, code_ref, upto_ref, left_ref, right_ref, out_ref,
+           left_all, right_all, lhs, rhs, sums, zsend, zrecv, lsend, psend, hsend, lrecv, hrecv, local_sem):
     row = lax.axis_index("row")
     col = lax.axis_index("col")
     q_count = right_ref.shape[0]
     left_blocks, blk = left_ref.shape[2], left_ref.shape[3]
     right_blocks = right_ref.shape[3]
-    step_count, pair_count = a_ref.shape
-    slot_count = last_ref.shape[1]
+    step_count, pair_count = code_ref.shape
+    slot_count = upto_ref.shape[1]
     groups = row_count // 2
     group, parity = row // 2, row % 2
     partner = group * 2 + 1 - parity
+    square = groups == 4
+    direct = (1, 2) if square else tuple(range(1, groups))
+
+    def group_at(i):
+        return (group // 2 * 2 + 1 - group % 2 if i == 1 else lax.rem(group + 2, groups)) if square and i in (1, 2) else (
+            groups - 1 - group if square and i == 3 else lax.rem(group + i, groups))
+
+    def row_at(i, same):
+        return group_at(i) * 2 + (parity if same else 1 - parity)
 
     barrier = pltpu.get_barrier_semaphore()
-    for i in range(1, groups):
-        peer = lax.rem(group + i, groups) * 2 + parity
-        pl.semaphore_signal(barrier, inc=1, device_id=(peer, col), device_id_type=MESH)
+    for i in direct:
+        pl.semaphore_signal(barrier, inc=1, device_id=(row_at(i, True), col), device_id_type=MESH)
     pl.semaphore_signal(barrier, inc=1, device_id=(partner, col), device_id_type=MESH)
 
     @pl.when(col > 0)
@@ -71,7 +69,7 @@
         copy.start()
 
     ends = (col == 0).astype(jnp.int32) + (col == col_count - 1).astype(jnp.int32)
-    pl.semaphore_wait(barrier, groups + 2 - ends)
+    pl.semaphore_wait(barrier, len(direct) + 3 - ends)
 
     def along(direction, q, source, from_ref):
         return pltpu.make_async_remote_copy(
@@ -95,12 +93,12 @@
             dst_ref=left_all.at[row],
             send_sem=lsend.at[i],
             recv_sem=lrecv.at[row],
-            device_id=(lax.rem(group + i, groups) * 2 + parity, col),
+            device_id=(row_at(i, True), col),
             device_id_type=MESH,
         )
 
     def handed(i):
-        source = lax.rem(group + i, groups) * 2 + parity
+        source = row_at(i, True)
         return pltpu.make_async_remote_copy(
             src_ref=left_ref.at[0, 0] if i == 0 else left_all.at[source],
             dst_ref=left_all.at[source],
@@ -120,6 +118,20 @@
             device_id_type=MESH,
         )
 
+    half = left_blocks // 2
+    pieces = (pl.ds(0, half), pl.ds(half, left_blocks - half))
+
+    def half_of(i, piece, target):
+        source = row_at(i, True)
+        return pltpu.make_async_remote_copy(
+            src_ref=left_all.at[source, pieces[piece]],
+            dst_ref=left_all.at[source, pieces[piece]],
+            send_sem=hsend.at[piece],
+            recv_sem=hrecv.at[piece],
+            device_id=(row_at(target, True), col),
+            device_id_type=MESH,
+        )
+
     for q in range(q_count):
         @pl.when(col > 0)
         def _():
@@ -129,7 +141,7 @@
         def _():
             own_panel(1, q).start()
 
-    for i in range(1, groups):
+    for i in direct:
         across(i).start()
     handed(0).start()
 
@@ -140,15 +152,19 @@
 
     sides = jnp.minimum(col, col_count - 1 - col)
 
-    def source_of(position):
-        rest = position - 1
-        distance = jnp.where(rest < 2 * sides, rest // 2 + 1, rest - sides + 1)
-        lower = jnp.where(rest < 2 * sides, rest % 2 == 0, col * 2 > col_count - 1)
-        shifted = jnp.where(lower, col - distance, col + distance)
-        return jnp.where(position == 0, col, shifted)
+    def item_of(item):
+        rest = item - q_count
+        later = rest - 2 * q_count * sides
+        both = later < 0
+        distance = jnp.where(both, rest // (2 * q_count) + 1, sides + 1 + later // q_count)
+        q = jnp.where(both, rest % (2 * q_count) // 2, later % q_count)
+        lower = jnp.where(both, rest % 2 == 0, col * 2 > col_count - 1)
+        source = jnp.where(lower, col - distance, col + distance)
+        own_item = rest < 0
+        return jnp.where(own_item, col, source), jnp.where(own_item, item, q)
 
     def relay(item):
-        source, q = source_of(item // q_count), lax.rem(item, q_count)
+        source, q = item_of(item)
 
         @pl.when(source != col)
         def _():
@@ -162,23 +178,27 @@
         def _():
             relayed(0, q, source).start()
 
-    first = min(2 * q_count, row_count)
-    lax.fori_loop(q_count, first, lambda item, c: (relay(item), c)[1], 0)
-    for i in range(1, groups):
-        source = lax.rem(group + i, groups) * 2 + parity
-        arrived_left(source).wait_recv()
+    forwards = 1 - ends
+    first = q_count * (2 + jnp.minimum(sides, 1))
+
+    def relay_many(start, stop):
+        lax.fori_loop(start, stop, lambda item, c: (relay(item), c)[1], 0)
+
+    for i in direct:
+        arrived_left(row_at(i, True)).wait_recv()
+        if square:
+            half_of(i, i - 1, 3 - i).start()
         handed(i).start()
+    relay_many(q_count, first)
+    if square:
+        half_of(3, 0, 1).wait_recv()
+        half_of(3, 1, 1).wait_recv()
+        handed(3).start()
     for i in range(groups):
-        arrived_left(lax.rem(group + i, groups) * 2 + 1 - parity).wait_recv()
+        arrived_left(row_at(i, False)).wait_recv()
 
     def job(item, carry):
-        ahead = item + AHEAD
-
-        @pl.when((ahead >= first) & (ahead < row_count))
-        def _():
-            relay(ahead)
-
-        source, q = source_of(item // q_count), lax.rem(item, q_count)
+        source, q = item_of(item)
         kgroup = q * col_count + source
         step = lax.rem(kgroup - row - col + 2 * row_count, row_count)
 
@@ -191,6 +211,16 @@
                 lhs[i, :, blk:] = (x - high.astype(jnp.float32)).astype(jnp.bfloat16)
                 return c
 
+            lax.fori_loop(0, left_blocks, split_left, 0)
+
+        ahead = item + AHEAD * forwards
+
+        @pl.when((ahead >= first) & (ahead < row_count))
+        def _():
+            relay(ahead)
+
+        @pl.when(step < step_count)
+        def _():
             def split_right(i, c):
                 x = right_all[q, source, i]
                 high = x.astype(jnp.bfloat16)
@@ -199,21 +229,29 @@
                 rhs[i, :blk, blk:] = (x - high.astype(jnp.float32)).astype(jnp.bfloat16)
                 return c
 
-            lax.fori_loop(0, left_blocks, split_left, 0)
             lax.fori_loop(0, right_blocks, split_right, 0)
 
-            def some(batch, total):
+            def some(batch, carry):
+                total, before = carry
                 for u in range(UNROLL):
                     p = batch * UNROLL + u
-                    both = jnp.dot(lhs[a_ref[step, p]], rhs[b_ref[step, p]], preferred_element_type=jnp.float32)
-                    total = total * keep_ref[step, p].astype(jnp.float32) + (both[:, :blk] + both[:, blk:])
+                    code = code_ref[step, p]
+                    both = jnp.dot(
+                        lhs[code & 255], rhs[(code >> 8) & 255], preferred_element_type=jnp.float32
+                    )
+                    slot = code >> 16
+                    keep = (slot == before).astype(jnp.float32)
+                    total = total * keep + (both[:, :blk] + both[:, blk:])
                     sums[p] = total
-                return total
-
-            lax.fori_loop(0, pair_count // UNROLL, some, jnp.zeros((blk, blk), jnp.float32))
+                    before = slot
+                return total, before
+
+            lax.fori_loop(0, pair_count // UNROLL, some, (jnp.zeros((blk, blk), jnp.float32), jnp.int32(-1)))
 
             def put(o, c):
-                out_ref[o] = out_ref[o] + sums[last_ref[step, o]] * valid_ref[step, o].astype(jnp.float32)
+                code = upto_ref[step, o]
+                found = ((code >> 16) > 0).astype(jnp.float32)
+                out_ref[o] = out_ref[o] + sums[jnp.maximum((code & 65535) - 1, 0)] * found
                 return c
 
             lax.fori_loop(0, slot_count, put, 0)
@@ -232,7 +270,7 @@
             own_panel(1, q).wait_send()
 
     def sent(item, carry):
-        source, q = source_of(item // q_count), lax.rem(item, q_count)
+        source, q = item_of(item)
 
         @pl.when((source < col) & (col < col_count - 1))
         def _():
@@ -245,8 +283,11 @@
         return carry
 
     lax.fori_loop(q_count, row_count, sent, 0)
-    for i in range(1, groups):
+    for i in direct:
         across(i).wait_send()
+    if square:
+        half_of(1, 0, 2).wait_send()
+        half_of(2, 1, 1).wait_send()
     for i in range(groups):
         handed(i).wait_send()
 
@@ -260,7 +301,7 @@
     out = pl.pallas_call(
         functools.partial(kernel, row_count, col_count),
         out_shape=jax.ShapeDtypeStruct((OCAP, blk, blk), jnp.float32),
-        in_specs=[pl.BlockSpec(memory_space=pltpu.SMEM)] * 5 + [pl.BlockSpec(memory_space=pl.ANY)] * 2,
+        in_specs=[pl.BlockSpec(memory_space=pltpu.SMEM)] * 2 + [pl.BlockSpec(memory_space=pl.ANY)] * 2,
         out_specs=pl.BlockSpec(memory_space=pltpu.VMEM),
         scratch_shapes=[
             pltpu.VMEM((row_count, left_blocks, blk, blk), jnp.float32),
@@ -272,7 +313,9 @@
             pltpu.SemaphoreType.DMA((q_count, col_count)),
             pltpu.SemaphoreType.DMA((groups,)),
             pltpu.SemaphoreType.DMA((groups,)),
+            pltpu.SemaphoreType.DMA((2,)),
             pltpu.SemaphoreType.DMA((row_count,)),
+            pltpu.SemaphoreType.DMA((2,)),
             pltpu.SemaphoreType.DMA((1 + q_count,)),
         ],
         compiler_params=pltpu.CompilerParams(

time: 158 us -> 120 us (0.76)
  Pallas kernels: 150 us -> 113 us
    pallas_call x1, Pallas kernels: 150 us -> 113 us  [shards(): pl.pallas_call(functools.partial(kernel, row_count, col_count), out_shape...]
where the time goes in v2:
time: 120 us
  Pallas kernels  113 us (94%)
  other arithmetic  4.07 us (3%)
  local copies, waits for them, and re-layouts  2.7 us (2%)
    pallas_call x1, Pallas kernels, shards(): pl.pallas_call(functools.partial(kernel, row_count, col_count), out_shape...  113 us
    unnamed x1, local copies, waits for them, and re-layouts  2.7 us

profile of v2, /device:TPU:0, one launch (start us, length us, event | category | flops | bytes accessed | tf_op | source)
XLA Modules:
  0.0 120.1 jit_solution(11481983119981623041)
XLA Ops:
  0.0 0.7 iota_add_fusion
  0.7 0.7 fusion.3
  1.4 0.8 add_reduce_fusion.upto_ref
  2.2 0.7 add_bitcast_fusion
  2.9 0.3 convert_reduce_fusion
  3.3 0.8 select_reduce_fusion.code_ref
  4.1 113.3 %shard_map.37 = f32[24,128,128]{2,1,0:T(8,128)} custom-call(s32[8,96]{1,0:T(8,128)} %select_reduce_fusion.code_ref, s32[8,24]{1,0:T(8,128)} %add_reduce_fusion.upto_ref, f32[1,1,16,128,128]{4,3,2,1,0:T(8,128)} %left_ref.1, f32[2,1,1,12,128,128]{5,4,3,2,1,0:T(8,128)} %right_ref.1), custom_call_target="tpu_custom_call" | custom-call | tf_op jit(solution)/shard_map/pallas_call | solution.py:301
  117.4 2.7 %copy.5 = f32[1,1,24,128,128]{4,3,2,1,0:T(8,128)} copy(f32[1,1,24,128,128]{4,3,2,1,0:T(8,128)} %bitcast.11) | data formatting | bytes 3145728

commit v3 on v2

--- a/solution.py
+++ b/solution.py
@@ -13,29 +13,38 @@
 MESH = pl.DeviceIdType.MESH
 
 
-def prepare(entries, slot_count):
-    count = entries.shape[1]
-    live = entries[..., 0] >= 0
-    slots = jnp.where(live, entries[..., 2], slot_count)
-    key = slots * count + jnp.arange(count, dtype=jnp.int32)
-    rank = jnp.sum((key[:, None, :] < key[:, :, None]).astype(jnp.int32), axis=2)
-    packed = jnp.where(live, entries[..., 0] + entries[..., 1] * 256, 0) + slots * 65536
-    place = rank[:, None, :] == jnp.arange(count, dtype=jnp.int32)[None, :, None]
-    codes = jnp.sum(jnp.where(place, packed[:, None, :], 0), axis=2)
-    ids = jnp.arange(slot_count, dtype=jnp.int32)[None, :, None]
-    upto = (slots[:, None, :] <= ids).astype(jnp.int32) + (slots[:, None, :] == ids).astype(jnp.int32) * 65536
-    return codes, jnp.sum(upto, axis=2)
-
-
-def kernel(row_count, col_count, code_ref, upto_ref, left_ref, right_ref, out_ref,
-           left_all, right_all, lhs, rhs, sums, zsend, zrecv, lsend, psend, hsend, lrecv, hrecv, local_sem):
+def arrange(lists_ref, table, step, slot_count):
+    step_count, count = lists_ref.shape[1], lists_ref.shape[2]
+    width = table.shape[1]
+    left, right, out = (lists_ref[part, pl.ds(step, 1), :] for part in range(3))
+    live = left >= 0
+    slots = jnp.where(live, out, slot_count)
+    lane = lax.broadcasted_iota(jnp.int32, (count, count), 1)
+    same = lax.broadcasted_iota(jnp.int32, (count, count), 0) == lane
+
+    def column(row):
+        return jnp.sum(jnp.where(same, jnp.broadcast_to(row, (count, count)), 0), axis=1, keepdims=True)
+
+    key = jnp.broadcast_to(slots, (count, count)) * count + lane
+    key_column = jnp.sum(jnp.where(same, key, 0), axis=1, keepdims=True)
+    rank = jnp.sum((key < key_column).astype(jnp.int32), axis=1, keepdims=True)
+    packed = column(jnp.where(live, left + right * 256, 0) + slots * 65536)
+    wide = lax.broadcasted_iota(jnp.int32, (count, width), 1)
+    table[pl.ds(step, 1), :] = jnp.sum(jnp.where(rank == wide, packed, 0), axis=0, keepdims=True)
+    slot_column = column(slots)
+    upto = (slot_column <= wide).astype(jnp.int32) + (slot_column == wide).astype(jnp.int32) * 65536
+    table[pl.ds(step_count + step, 1), :] = jnp.sum(upto, axis=0, keepdims=True)
+
+
+def kernel(row_count, col_count, lists_ref, left_ref, right_ref, out_ref,
+           left_all, right_all, lhs, rhs, sums, table, code_ref, zsend, zrecv, lsend, psend, hsend, lrecv, hrecv, local_sem):
     row = lax.axis_index("row")
     col = lax.axis_index("col")
     q_count = right_ref.shape[0]
     left_blocks, blk = left_ref.shape[2], left_ref.shape[3]
     right_blocks = right_ref.shape[3]
-    step_count, pair_count = code_ref.shape
-    slot_count = upto_ref.shape[1]
+    step_count, pair_count = lists_ref.shape[1], lists_ref.shape[2]
+    slot_count = out_ref.shape[0]
     groups = row_count // 2
     group, parity = row // 2, row % 2
     partner = group * 2 + 1 - parity
@@ -145,6 +154,7 @@
         across(i).start()
     handed(0).start()
 
+    lax.fori_loop(0, step_count, lambda step, c: (arrange(lists_ref, table, step, slot_count), c)[1], 0)
     out_ref[...] = jnp.zeros_like(out_ref)
     rhs[:, blk:, blk:] = jnp.zeros((right_blocks, blk, blk), rhs.dtype)
     for copy in own:
@@ -190,12 +200,15 @@
             half_of(i, i - 1, 3 - i).start()
         handed(i).start()
     relay_many(q_count, first)
+    listed = pltpu.make_async_copy(table, code_ref, local_sem.at[1 + q_count])
+    listed.start()
     if square:
         half_of(3, 0, 1).wait_recv()
         half_of(3, 1, 1).wait_recv()
         handed(3).start()
     for i in range(groups):
         arrived_left(row_at(i, False)).wait_recv()
+    listed.wait()
 
     def job(item, carry):
         source, q = item_of(item)
@@ -249,7 +262,7 @@
             lax.fori_loop(0, pair_count // UNROLL, some, (jnp.zeros((blk, blk), jnp.float32), jnp.int32(-1)))
 
             def put(o, c):
-                code = upto_ref[step, o]
+                code = code_ref[step_count + step, o]
                 found = ((code >> 16) > 0).astype(jnp.float32)
                 out_ref[o] = out_ref[o] + sums[jnp.maximum((code & 65535) - 1, 0)] * found
                 return c
@@ -296,12 +309,14 @@
     left_blocks, blk = left_panels.shape[2], left_panels.shape[3]
     q_count, right_blocks = right_panels.shape[0], right_panels.shape[3]
     pair_count = product_lists.shape[3]
-    lists = prepare(product_lists[0, 0], OCAP)
+    lists = jnp.transpose(product_lists[0, 0], (2, 0, 1))
+    step_count = lists.shape[1]
+    width = pl.cdiv(max(pair_count, OCAP), 128) * 128
     groups = row_count // 2
     out = pl.pallas_call(
         functools.partial(kernel, row_count, col_count),
         out_shape=jax.ShapeDtypeStruct((OCAP, blk, blk), jnp.float32),
-        in_specs=[pl.BlockSpec(memory_space=pltpu.SMEM)] * 2 + [pl.BlockSpec(memory_space=pl.ANY)] * 2,
+        in_specs=[pl.BlockSpec(memory_space=pltpu.VMEM)] + [pl.BlockSpec(memory_space=pltpu.HBM)] * 2,
         out_specs=pl.BlockSpec(memory_space=pltpu.VMEM),
         scratch_shapes=[
             pltpu.VMEM((row_count, left_blocks, blk, blk), jnp.float32),
@@ -309,6 +324,8 @@
             pltpu.VMEM((left_blocks, blk, 2 * blk), jnp.bfloat16),
             pltpu.VMEM((right_blocks, 2 * blk, 2 * blk), jnp.bfloat16),
             pltpu.VMEM((pair_count, blk, blk), jnp.float32),
+            pltpu.VMEM((2 * step_count, width), jnp.int32),
+            pltpu.SMEM((2 * step_count, width), jnp.int32),
             pltpu.SemaphoreType.DMA((2, q_count, col_count)),
             pltpu.SemaphoreType.DMA((q_count, col_count)),
             pltpu.SemaphoreType.DMA((groups,)),
@@ -316,12 +333,12 @@
             pltpu.SemaphoreType.DMA((2,)),
             pltpu.SemaphoreType.DMA((row_count,)),
             pltpu.SemaphoreType.DMA((2,)),
-            pltpu.SemaphoreType.DMA((1 + q_count,)),
+            pltpu.SemaphoreType.DMA((2 + q_count,)),
         ],
         compiler_params=pltpu.CompilerParams(
-            collective_id=0, has_side_effects=True, vmem_limit_bytes=60 * 1024 * 1024
+            collective_id=0, has_side_effects=True, vmem_limit_bytes=50 * 1024 * 1024
         ),
-    )(*lists, left_panels, right_panels)
+    )(lists, left_panels, right_panels)
     return out[None, None]
 
 

time: 120 us -> 115 us (0.958)
  other arithmetic: 4.07 us -> 0 us
  Pallas kernels: 113 us -> 111 us
    pallas_call x1, Pallas kernels: 113 us -> 111 us  [shards(): pl.pallas_call(functools.partial(kernel, row_count, col_count), out_shape...]
    reduce_sum x3 -> x0, other arithmetic: 1.97 us -> none  [the longest x1 0.81 us: prepare(): codes = jnp.sum(jnp.where(place, packed[:, None, :], 0), axis=2)]
    add x2 -> x0, other arithmetic: 1.42 us -> none  [the longest x1 0.71 us: prepare(): jnp.where(live, entries[..., 0] + entries[..., 1] * 256, 0) + slots * 65536]
    unnamed x1 -> x5, local copies, waits for them, and re-layouts: 2.7 us -> 3.08 us
where the time goes in v3:
time: 115 us; the launch traced here: 114 us
  Pallas kernels  111 us (97%)
  local copies, waits for them, and re-layouts  3.08 us (3%)
    pallas_call x1, Pallas kernels, shards(): pl.pallas_call(functools.partial(kernel, row_count, col_count), out_shape...  111 us
    unnamed x5, local copies, waits for them, and re-layouts  3.08 us

profile of v3, /device:TPU:0, one launch (start us, length us, event | category | flops | bytes accessed | tf_op | source)
XLA Modules:
  0.0 114.4 jit_solution(17388606026206940019)
XLA Ops:
  0.0 0.0 copy-start
  0.0 1.2 %copy-done = f32[1,1,16,128,128]{4,3,2,1,0:T(8,128)S(1)} copy-done((f32[1,1,16,128,128]{4,3,2,1,0:T(8,128)S(1)}, f32[1,1,16,128,128]{4,3,2,1,0:T(8,128)}, u32[]{:S(2)}) %copy-start) | copy-done | bytes 1048600
  1.2 0.0 copy-start.1
  1.2 0.7 copy-done.1
  1.9 111.3 %shard_map.37 = f32[24,128,128]{2,1,0:T(8,128)S(1)} custom-call(s32[3,8,96]{2,1,0:T(8,128)S(1)} %bitcast.5, f32[1,1,16,128,128]{4,3,2,1,0:T(8,128)S(1)} %copy-done, f32[2,1,1,12,128,128]{5,4,3,2,1,0:T(8,128)} %right_ref.1), custom_call_target="tpu_custom_call" | custom-call | tf_op jit(solution)/shard_map/pallas_call | solution.py:316
  113.3 1.1 %copy.5 = f32[1,1,24,128,128]{4,3,2,1,0:T(8,128)} copy(f32[1,1,24,128,128]{4,3,2,1,0:T(8,128)S(1)} %bitcast.4) | data formatting | bytes 3145728
Async XLA Ops:
  0.0 1.2 %copy-start = (f32[1,1,16,128,128]{4,3,2,1,0:T(8,128)S(1)}, f32[1,1,16,128,128]{4,3,2,1,0:T(8,128)}, u32[]{:S(2)}) copy-start(f32[1,1,16,128,128]{4,3,2,1,0:T(8,128)} %left_ref.1) | copy-start | bytes 3145732
  1.2 0.7 copy-start.1

commit v4 on v3

--- a/solution.py
+++ b/solution.py
@@ -8,7 +8,7 @@
 from jax.sharding import PartitionSpec as P
 
 OCAP = 24
-UNROLL = 8
+UNROLL = 16
 AHEAD = 3
 MESH = pl.DeviceIdType.MESH
 

time: 115 us -> 114 us (level)
  no operation moved by 1% of the time
where the time goes in v4:
time: 114 us; the launch traced here: 113 us
  Pallas kernels  110 us (96%)
  local copies, waits for them, and re-layouts  3.08 us (3%)
    pallas_call x1, Pallas kernels, shards(): pl.pallas_call(functools.partial(kernel, row_count, col_count), out_shape...  110 us
    unnamed x5, local copies, waits for them, and re-layouts  3.08 us

profile of v4, /device:TPU:0, one launch (start us, length us, event | category | flops | bytes accessed | tf_op | source)
XLA Modules:
  0.0 113.4 jit_solution(11783118805431402602)
XLA Ops:
  0.0 0.0 copy-start
  0.0 1.2 %copy-done = f32[1,1,16,128,128]{4,3,2,1,0:T(8,128)S(1)} copy-done((f32[1,1,16,128,128]{4,3,2,1,0:T(8,128)S(1)}, f32[1,1,16,128,128]{4,3,2,1,0:T(8,128)}, u32[]{:S(2)}) %copy-start) | copy-done | bytes 1048600
  1.2 0.0 copy-start.1
  1.2 0.7 copy-done.1
  1.9 110.3 %shard_map.37 = f32[24,128,128]{2,1,0:T(8,128)S(1)} custom-call(s32[3,8,96]{2,1,0:T(8,128)S(1)} %bitcast.5, f32[1,1,16,128,128]{4,3,2,1,0:T(8,128)S(1)} %copy-done, f32[2,1,1,12,128,128]{5,4,3,2,1,0:T(8,128)} %right_ref.1), custom_call_target="tpu_custom_call" | custom-call | tf_op jit(solution)/shard_map/pallas_call | solution.py:316
  112.2 1.1 %copy.5 = f32[1,1,24,128,128]{4,3,2,1,0:T(8,128)} copy(f32[1,1,24,128,128]{4,3,2,1,0:T(8,128)S(1)} %bitcast.4) | data formatting | bytes 3145728
Async XLA Ops:
  0.0 1.2 %copy-start = (f32[1,1,16,128,128]{4,3,2,1,0:T(8,128)S(1)}, f32[1,1,16,128,128]{4,3,2,1,0:T(8,128)}, u32[]{:S(2)}) copy-start(f32[1,1,16,128,128]{4,3,2,1,0:T(8,128)} %left_ref.1) | copy-start | bytes 3145732
  1.2 0.7 copy-start.1
